TPU v7x, 256 devices: a whole 4x4x8 slice. The times are simulated.
256 devices in a mesh: seq: 32 (over z, x), head: 8 (over y, core).
Axes of the slice: x: 4, y: 4, z: 8, core: 2. Of those that a mesh axis runs over, the one named last changes fastest.
Arguments:
- corpus: bfloat16 [128, 128, 4096], P('seq'), may hold values from -8 to 8
- enc_qkv: bfloat16 [4096, 16, 3, 128], P(None, 'head'), may hold values from -0.1015625 to 0.1015625
- enc_out: bfloat16 [16, 128, 4096], P('head'), may hold values from -0.375 to 0.375
- cca_kv: bfloat16 [4096, 16, 2, 128], P('seq', 'head'), may hold values from -0.09375 to 0.09375
- gain_in: float32 [4096], replicated, may hold values from 0.5 to 2
- gain_out: float32 [4096], replicated, may hold values from 0.5 to 2
- queries: bfloat16 [16384, 16, 128], P('seq', 'head'), may hold values from -100 to 100
- nbr_ids: int32 [256, 2], P('seq'), may hold values from 0 to 127, as said below
Outputs:
- cca_out: bfloat16 [16384, 16, 128], P('seq', 'head')
Inputs may be any that keep to these rules, and one draw needn't show every extreme that they name: `nbr_ids`: entry [u, n] is the corpus row of group u's n-th neighbour; row r is held by index r // 4 of seq. The neighbours of one group differ. Among the requests of the 8 groups of one index of seq no owner is named more than 2 times, and in every draw some owner is named exactly 2 times by every index of seq.
All inputs are finite; a program needn't handle non-finite values.
Results may differ from a plain program's by a relative error of at most 0.03.
Values may be sent and summed in bfloat16 or wider, within the bound.
No kernel may reach another device: no remote copies, remote signals or barrier semaphores. Data moves between devices by JAX's collectives and lax.ppermute only.
A program may use at most 128 MiB of HBM per device.

v0:
```python
import jax
import jax.numpy as jnp
from jax import lax
from jax.sharding import PartitionSpec as P

GROUP = 64
NBRS = 2
CAP = 2
EPS = 1e-06


def passed_along(value, axis, steps):
    count = lax.axis_size(axis)
    first, last = (max(0, -steps), min(count, count - steps))
    return lax.ppermute(value, axis, [(source, source + steps) for source in range(first, last)])


def rms_scale(values, gain):
    mean_square = jnp.mean(values * values, axis=-1, keepdims=True)
    return values * lax.rsqrt(mean_square + EPS) * gain


def attend(query_blocks, key_blocks, value_blocks):
    scale = query_blocks.shape[-1] ** (-0.5)
    scores = (
        jnp.einsum("bqhs,bkhs->bhqk", query_blocks, key_blocks, preferred_element_type=jnp.float32)
        * scale
    )
    probs = jax.nn.softmax(scores, axis=-1).astype(jnp.bfloat16)
    return jnp.einsum("bhqk,bkhs->bqhs", probs, value_blocks, preferred_element_type=jnp.float32)


def on_device(corpus, enc_qkv, enc_out, cca_kv, gain_in, gain_out, queries, nbr_ids):
    corp_rows, row_tokens, model_width = corpus.shape
    heads_here = enc_qkv.shape[1]
    head_size = enc_qkv.shape[3]
    row_total = corp_rows * row_tokens
    corpus_flat = corpus.reshape(row_total, model_width)
    normed_in = rms_scale(corpus_flat.astype(jnp.float32), gain_in).astype(jnp.bfloat16)
    projected = jnp.dot(
        normed_in,
        enc_qkv.reshape(model_width, heads_here * 3 * head_size),
        preferred_element_type=jnp.float32,
    )
    projected = projected.astype(jnp.bfloat16).reshape(
        corp_rows, row_tokens, heads_here, 3, head_size
    )
    attended = attend(projected[:, :, :, 0], projected[:, :, :, 1], projected[:, :, :, 2]).astype(
        jnp.bfloat16
    )
    attended = attended.reshape(row_total, heads_here * head_size)
    out_weight = enc_out.reshape(heads_here * head_size, model_width)
    partial_terms = jnp.dot(attended, out_weight, preferred_element_type=jnp.float32)
    enc_sum = lax.psum(partial_terms, "head")
    normed = rms_scale(corpus_flat.astype(jnp.float32) + enc_sum, gain_out).astype(jnp.bfloat16)
    memory_cols = heads_here * 2 * head_size
    shard_piece = lax.all_gather(cca_kv, "seq", axis=0, tiled=True)
    memory = jnp.dot(
        normed,
        shard_piece.reshape(shard_piece.shape[0], memory_cols),
        preferred_element_type=jnp.float32,
    )
    memory = memory.astype(jnp.bfloat16).reshape(corp_rows, row_tokens, heads_here, 2, head_size)
    request_ids = nbr_ids.reshape(-1)
    demand = request_ids.shape[0]
    owners = request_ids // corp_rows
    local_row = request_ids % corp_rows
    request_order = jnp.arange(demand)
    earlier = request_order[None, :] < request_order[:, None]
    same_owner = owners[:, None] == owners[None, :]
    slot_rank = jnp.sum(jnp.logical_and(same_owner, earlier), axis=1)
    slot_index = owners * CAP + slot_rank
    devices = lax.axis_size("seq")
    positions = jnp.arange(devices * CAP)
    matched = positions[:, None] == slot_index[None, :]
    wanted = jnp.sum(jnp.where(matched, local_row[None, :], 0), axis=1).reshape(devices, CAP)
    picked = jnp.take(
        memory, lax.all_to_all(wanted, "seq", split_axis=0, concat_axis=0, tiled=True), axis=0
    )
    fetched = lax.all_to_all(picked, "seq", split_axis=0, concat_axis=0, tiled=True)
    fetched = fetched.reshape(devices * CAP, row_tokens, heads_here, 2, head_size)
    group_memory = jnp.take(fetched, slot_index, axis=0)
    groups_here = nbr_ids.shape[0]
    group_memory = group_memory.reshape(groups_here, NBRS * row_tokens, heads_here, 2, head_size)
    token_count = queries.shape[0]
    lead = GROUP - 1
    before = passed_along(group_memory[groups_here - 1 :], "seq", 1)
    window_memory = jnp.concatenate([before, group_memory], axis=0)
    padded_queries = jnp.concatenate(
        [
            jnp.zeros((1, heads_here, head_size), jnp.bfloat16),
            queries,
            jnp.zeros((lead, heads_here, head_size), jnp.bfloat16),
        ],
        axis=0,
    ).reshape(groups_here + 1, GROUP, heads_here, head_size)
    extended = attend(padded_queries, window_memory[:, :, :, 0], window_memory[:, :, :, 1])
    extended = extended.reshape((groups_here + 1) * GROUP, heads_here, head_size)
    result = extended[1 : 1 + token_count].astype(jnp.bfloat16)
    return result


def solution(mesh):
    placed = (
        P("seq", None, None),
        P(None, "head", None, None),
        P("head", None, None),
        P("seq", "head", None, None),
        P(),
        P(),
        P("seq", "head", None),
        P("seq", None),
    )
    return jax.shard_map(
        on_device, mesh=mesh, in_specs=placed, out_specs=P("seq", "head", None), check_vma=False
    )
```

profile of v0, /device:TPU:104, one launch (start us, length us, event | category | flops | bytes accessed | tf_op | source)
XLA Modules:
  0.0 442.4 jit_solution(8818635364731222058)
XLA Ops:
  7.4 16.4 %copy.108 = bf16[4096,2,3,128]{0,3,2,1:T(8,128)(2,1)} copy(bf16[4096,2,3,128]{3,1,2,0:T(2,128)(2,1)} %param.9) | data formatting | bytes 12582912 | tf_op args[1]
  23.8 3.2 multiply_reduce_fusion.1
  27.0 0.2 copy-done.2
  27.2 1.7 multiply_convert_fusion.1
  28.9 1.1 copy-done.3
  30.0 3.5 convolution_convert_fusion
  33.5 1.2 copy.109
  34.6 1.7 reshape.286
  36.4 1.0 fusion.50
  37.4 0.2 copy.129
  37.6 0.2 copy.130
  37.8 0.3 convolution_multiply_fusion.1
  38.1 0.4 fusion.51
  38.5 1.3 fusion.19
  39.7 0.2 copy.114
  39.9 4.5 %fusion.22 = f32[512,4096]{1,0:T(8,128)} fusion(bf16[256,4096]{1,0:T(8,128)(2,1)S(1)} %bitcast.79, bf16[64,8,2,128]{3,2,1,0:T(2,128)(2,1)S(1)} %bitcast.85), kind=kOutput, calls=%fused_computation.38 | convolution fusion | flops 1073741824 | bytes 10747904 | tf_op jit(solution)/shard_map/dot_general | solution.py:53
  44.5 0.5 all-gather.2.cloned.1.call-update
  45.1 0.1 copy.104
  45.2 0.1 reshape.284
  45.3 0.2 convert_reduce_fusion
  45.5 0.1 select_reduce_fusion
  45.5 0.1 all_to_all.13
  45.7 16.9 %all_to_all.20 = s32[32,1,2]{2,1,0:T(1,128)S(1)} all-to-all(s32[32,1,2]{2,1,0:T(1,128)S(1)} %bitcast.88), channel_id=1, replica_groups=mesh['seq'=32,'head'=8] {'seq'}, dimensions={0} | all-to-all | bytes 512 | tf_op jit(solution)/shard_map/all_to_all | solution.py:78
  62.6 0.1 copy.116
  62.7 0.1 reshape.298
  62.9 0.1 copy.107
  63.0 90.3 %all-reduce.2.cloned.1.call-done = f32[512,4096]{1,0:T(8,128)} async-done(((f32[512,4096]{1,0:T(8,128)}), f32[512,4096]{1,0:T(8,128)}) %all-reduce.2.cloned.1.call-update) | async-done | bytes 8388624 | tf_op jit(solution)/shard_map/psum | solution.py:54
  153.3 8.9 %multiply_reduce_fusion = (f32[512]{0:T(512)S(1)}, f32[512,4096]{1,0:T(8,128)}) fusion(f32[512,4096]{1,0:T(8,128)} %all-reduce.2.cloned.1.call-done, bf16[4,128,4096]{2,1,0:T(8,128)(2,1)} %param.8), kind=kLoop, calls=%fused_computation.7 | loop fusion | flops 8388096 | bytes 20973568 | tf_op jit(solution)/shard_map/reduce_sum | solution.py:19
  162.2 7.2 %reshape.289 = bf16[4096,512]{1,0:T(8,128)(2,1)} reshape(bf16[4096,2,2,128]{3,2,1,0:T(2,128)(2,1)} %all-gather.2.cloned.1.call-done) | data formatting | bytes 8388608 | tf_op jit(solution)/shard_map/reshape | solution.py:60
  169.4 6.9 %fusion.7 = bf16[512,512]{1,0:T(8,128)(2,1)S(1)} fusion(bf16[4096,512]{1,0:T(8,128)(2,1)} %reshape.289, f32[512,4096]{1,0:T(8,128)} %get-tuple-element.8, f32[4096]{0:T(1024)S(1)} %copy-done.7, f32[512]{0:T(512)S(1)} %add_rsqrt_fusion), kind=kOutput, calls=%fused_computation.20 | convolution fusion | flops 2154037248 | bytes 13125632 | tf_op jit(solution)/shard_map/dot_general | solution.py:58
  176.3 0.1 reshape.290
  176.5 18.3 %gather_fusion = bf16[64,128,2,2,128]{4,3,2,1,0:T(2,128)(2,1)} fusion(bf16[4,128,2,2,128]{4,3,2,1,0:T(2,128)(2,1)S(1)} %reshape.290, s32[1024]{0:T(1024)S(1)} %pad_clamp_fusion.1), kind=kCustom, calls=%fused_computation | custom fusion | bytes 16777472 | tf_op jit(solution)/shard_map/jit(_take)/gather | solution.py:77
  194.8 7.7 %copy_select_fusion = bf16[32,2,128,2,2,128]{5,2,4,3,1,0:T(8,128)(2,1)} fusion(bf16[32,2,128,2,2,128]{5,4,3,2,1,0:T(2,128)(2,1)} %bitcast.80, pred[32,2]{1,0:T(8,128)(4,1)S(1)} %copy.107), kind=kLoop, calls=%fused_computation.5 | loop fusion | flops 4194304 | bytes 16777280 | tf_op jit(solution)/shard_map/jit(_take)/select_n | solution.py:77
  202.6 10.0 %all-to-all-start.1 = ((bf16[32,2,128,2,2,128]{5,2,4,3,1,0:T(8,128)(2,1)}), bf16[32,2,128,2,2,128]{5,2,4,3,1,0:T(8,128)(2,1)}, u32[]{:S(2)}, u32[]{:S(2)}) async-start(bf16[32,2,128,2,2,128]{5,2,4,3,1,0:T(8,128)(2,1)} %copy_select_fusion), calls=%async_computation.1 | async-start | bytes 16777216 | tf_op jit(solution)/shard_map/all_to_all | solution.py:80
  212.6 0.1 reshape.292
  212.7 0.1 reduce_sum.64
  212.8 0.1 copy.120
  213.2 0.2 maximum_maximum_fusion
  213.4 198.6 %all-to-all-done.1 = bf16[32,2,128,2,2,128]{5,2,4,3,1,0:T(8,128)(2,1)} async-done(((bf16[32,2,128,2,2,128]{5,2,4,3,1,0:T(8,128)(2,1)}), bf16[32,2,128,2,2,128]{5,2,4,3,1,0:T(8,128)(2,1)}, u32[]{:S(2)}, u32[]{:S(2)}) %all-to-all-start.1) | async-done | bytes 8388640 | tf_op jit(solution)/shard_map/all_to_all | solution.py:80
  412.0 4.3 gather_fusion.1
  416.3 0.1 copy.121
  416.4 0.1 slice_select_fusion
  416.6 1.9 collective-permute-start
  418.5 1.6 copy_select_fusion.1
  420.1 8.8 %collective-permute-done = bf16[1,256,2,2,128]{4,1,2,0,3:T(8,128)(2,1)S(1)} collective-permute-done((bf16[1,256,2,2,128]{4,1,2,0,3:T(8,128)(2,1)S(1)}, bf16[1,256,2,2,128]{4,1,2,0,3:T(8,128)(2,1)S(1)}, u32[]{:S(2)}, u32[]{:S(2)}) %collective-permute-start) | collective-permute-done | bytes 262176 | tf_op jit(solution)/shard_map/ppermute | solution.py:15
  428.8 3.1 fusion.56
  431.9 2.0 fusion.16
  434.0 1.0 copy.126
  (38 shorter events, 0.7 us)
Async XLA Ops:
  7.4 32.6 %copy-start = (bf16[2,128,4096]{2,1,0:T(8,128)(2,1)S(1)}, bf16[2,128,4096]{2,1,0:T(8,128)(2,1)}, u32[]{:S(2)}) copy-start(bf16[2,128,4096]{2,1,0:T(8,128)(2,1)} %param.10) | copy-start | bytes 6291460
  7.4 145.9 %all-reduce.2.cloned.1.call-start = ((), (), s32[]{:S(2)}) async-start(), calls=%async_computation.2 | async-start | bytes 16777216 | tf_op jit(solution)/shard_map/psum | solution.py:54
  7.4 19.6 %copy-start.5 = (f32[4096]{0:T(1024)S(1)}, f32[4096]{0:T(1024)}, u32[]{:S(2)}) copy-start(f32[4096]{0:T(1024)} %param.12) | copy-start | bytes 49156
  23.8 3.4 copy-start.2
  27.2 2.8 copy-start.3
  44.4 0.7 copy-start.6
  44.4 117.7 %all-gather.2.cloned.1.call-start = ((), (), s32[]{:S(2)}) async-start(), calls=%async_computation.3 | async-start | bytes 4325376 | tf_op jit(solution)/shard_map/all_gather | solution.py:57
  162.1 7.3 %copy-start.7 = (f32[4096]{0:T(1024)S(1)}, f32[4096]{0:T(1024)}, u32[]{:S(2)}) copy-start(f32[4096]{0:T(1024)} %param.13) | copy-start | bytes 49156
  202.6 10.3 %copy-start.4 = (bf16[512,2,128]{2,1,0:T(2,128)(2,1)S(1)}, bf16[512,2,128]{2,1,0:T(2,128)(2,1)}, u32[]{:S(2)}) copy-start(bf16[512,2,128]{2,1,0:T(2,128)(2,1)} %param.14) | copy-start | bytes 786436
  202.6 209.4 %all-to-all-start.1 = ((bf16[32,2,128,2,2,128]{5,2,4,3,1,0:T(8,128)(2,1)}), bf16[32,2,128,2,2,128]{5,2,4,3,1,0:T(8,128)(2,1)}, u32[]{:S(2)}, u32[]{:S(2)}) async-start(bf16[32,2,128,2,2,128]{5,2,4,3,1,0:T(8,128)(2,1)} %copy_select_fusion), calls=%async_computation.1 | async-start | bytes 16777216 | tf_op jit(solution)/shard_map/all_to_all | solution.py:80
  416.6 12.3 %collective-permute-start = (bf16[1,256,2,2,128]{4,1,2,0,3:T(8,128)(2,1)S(1)}, bf16[1,256,2,2,128]{4,1,2,0,3:T(8,128)(2,1)S(1)}, u32[]{:S(2)}, u32[]{:S(2)}) collective-permute-start(bf16[1,256,2,2,128]{4,1,2,0,3:T(8,128)(2,1)S(1)} %bitcast.87), channel_id=1, source_target_pairs={{0,8},{8,16},{16,24},{24,32},{32,40},{40,48},{48,56},{56,64},{64,7... | collective-permute-start | bytes 786440 | tf_op jit(solution)/shard_map/ppermute | solution.py:15
  428.8 6.1 %copy-start.1 = (bf16[2,128,4096]{2,1,0:T(8,128)(2,1)S(1)}, bf16[2,128,4096]{2,1,0:T(8,128)(2,1)}, u32[]{:S(2)}) copy-start(bf16[2,128,4096]{2,1,0:T(8,128)(2,1)} %param.10) | copy-start | bytes 6291460
Sparse Core Ops, SparseCore 0:
  44.6 108.6 all-reduce.1
Sparse Core Ops, SparseCore 1:
  47.5 83.2 all-gather.1
where the time goes:
time: 443 us; the launch traced here: 442 us
  waiting for transfers between devices  298 us (67%)
  local copies, waits for them, and re-layouts  54.6 us (12%)
  other arithmetic  23.7 us (5%)
  matrix products  21.9 us (5%)
  blocking collectives  16.9 us (4%)
  between operations  15.1 us (3%)
  starting transfers between devices  12 us (3%)
    all_to_all x1, waiting for transfers between devices, on_device(): lax.all_to_all(picked, 'seq', split_axis=0, concat_axis=0, tiled=True)  199 us
    psum x1, waiting for transfers between devices, on_device(): enc_sum = lax.psum(partial_terms, 'head')  90.3 us
    unnamed x21, local copies, waits for them, and re-layouts  18.3 us
    gather x1, local copies, waits for them, and re-layouts, on_device(): jnp.take(memory, lax.all_to_all(wanted, 'seq', split_axis=0, concat_axis=...  18.3 us
    all_to_all x1, blocking collectives, on_device(): lax.all_to_all(wanted, 'seq', split_axis=0, concat_axis=0, tiled=True)  16.9 us
    reduce_sum x2, other arithmetic, rms_scale(): mean_square = jnp.mean(values * values, axis=-1, keepdims=True)  12.1 us
    all_to_all x1, starting transfers between devices, on_device(): lax.all_to_all(picked, 'seq', split_axis=0, concat_axis=0, tiled=True)  10 us
  transfers between devices with their start and end apart: 4, of which 3 were waited for; matrix products, arithmetic and copies ran while one was open for 3% of the time, Pallas kernels for 0%

commit v1 on v0

--- a/solution.py
+++ b/solution.py
@@ -51,7 +51,9 @@
     attended = attended.reshape(row_total, heads_here * head_size)
     out_weight = enc_out.reshape(heads_here * head_size, model_width)
     partial_terms = jnp.dot(attended, out_weight, preferred_element_type=jnp.float32)
-    enc_sum = lax.psum(partial_terms, "head")
+    enc_sum = partial_terms
+    for hop in (1, 2, 4):
+        enc_sum = enc_sum + lax.ppermute(enc_sum, "head", [(dev, dev ^ hop) for dev in range(8)])
     normed = rms_scale(corpus_flat.astype(jnp.float32) + enc_sum, gain_out).astype(jnp.bfloat16)
     memory_cols = heads_here * 2 * head_size
     shard_piece = lax.all_gather(cca_kv, "seq", axis=0, tiled=True)

time: 443 us -> 709 us (1.60); the launches traced: 442 us -> 701 us
  waiting for transfers between devices: 298 us -> 536 us
  other arithmetic: 23.7 us -> 45.3 us
  matrix products: 21.9 us -> 14 us
    ppermute x0 -> x3, waiting for transfers between devices: none -> 287 us  [on_device(): lax.ppermute(enc_sum, 'head', [(dev, dev ^ hop) for dev in range(8)])]
    psum x1 -> x0, waiting for transfers between devices: 90.3 us -> none  [on_device(): enc_sum = lax.psum(partial_terms, 'head')]
    all_gather x1, waiting for transfers between devices: 0.02 us -> 64.4 us  [on_device(): shard_piece = lax.all_gather(cca_kv, 'seq', axis=0, tiled=True)]
    add x0 -> x2, other arithmetic: none -> 22.2 us  [on_device(): enc_sum + lax.ppermute(enc_sum, 'head', [(dev, dev ^ hop) for dev in rang...]
    all_to_all x1, waiting for transfers between devices: 199 us -> 179 us  [on_device(): lax.all_to_all(picked, 'seq', split_axis=0, concat_axis=0, tiled=True)]
    unnamed x21 -> x25, local copies, waits for them, and re-layouts: 18.3 us -> 21.5 us
  transfers between devices with their start and end apart: 4 -> 6, of which waited for: 3 -> 6; matrix products, arithmetic and copies ran while one was open for 3% -> 1% of each run, Pallas kernels for 0% -> 0%
where the time goes in v1:
time: 709 us; the launch traced here: 701 us
  waiting for transfers between devices  536 us (76%)
  local copies, waits for them, and re-layouts  57.8 us (8%)
  other arithmetic  45.3 us (6%)
  blocking collectives  16.9 us (2%)
  starting transfers between devices  16.5 us (2%)
  matrix products  14 us (2%)
  between operations  13.7 us (2%)
    ppermute x3, waiting for transfers between devices, on_device(): lax.ppermute(enc_sum, 'head', [(dev, dev ^ hop) for dev in range(8)])  287 us
    all_to_all x1, waiting for transfers between devices, on_device(): lax.all_to_all(picked, 'seq', split_axis=0, concat_axis=0, tiled=True)  179 us
    all_gather x1, waiting for transfers between devices, on_device(): shard_piece = lax.all_gather(cca_kv, 'seq', axis=0, tiled=True)  64.4 us
    add x2, other arithmetic, on_device(): enc_sum + lax.ppermute(enc_sum, 'head', [(dev, dev ^ hop) for dev in rang...  22.2 us
    unnamed x25, local copies, waits for them, and re-layouts  21.5 us
    gather x1, local copies, waits for them, and re-layouts, on_device(): jnp.take(memory, lax.all_to_all(wanted, 'seq', split_axis=0, concat_axis=...  18.3 us
    all_to_all x1, blocking collectives, on_device(): lax.all_to_all(wanted, 'seq', split_axis=0, concat_axis=0, tiled=True)  16.9 us
  transfers between devices with their start and end apart: 6, of which 6 were waited for; matrix products, arithmetic and copies ran while one was open for 1% of the time, Pallas kernels for 0%

profile of v1, /device:TPU:104, one launch (start us, length us, event | category | flops | bytes accessed | tf_op | source)
XLA Modules:
  0.0 700.5 jit_solution(12309918819749419952)
XLA Ops:
  6.5 16.4 %copy.108 = bf16[4096,2,3,128]{0,3,2,1:T(8,128)(2,1)} copy(bf16[4096,2,3,128]{3,1,2,0:T(2,128)(2,1)} %param.9) | data formatting | bytes 12582912 | tf_op args[1]
  22.9 3.2 multiply_reduce_fusion.1
  26.2 0.2 copy-done.2
  26.4 1.7 multiply_convert_fusion.1
  28.0 1.1 copy-done.4
  29.2 3.5 convolution_convert_fusion
  32.6 1.2 copy.109
  33.8 1.7 reshape.286
  35.6 1.0 fusion.50
  36.5 0.2 copy.129
  36.7 0.2 copy.130
  37.0 0.3 convolution_multiply_fusion.1
  37.3 0.4 fusion.51
  37.6 1.3 fusion.19
  38.9 0.2 copy.114
  39.1 1.3 fusion.22
  40.4 3.2 copy-done.3
  43.6 13.3 %collective-permute-done = f32[512,4096]{1,0:T(8,128)} collective-permute-done((f32[512,4096]{1,0:T(8,128)S(1)}, f32[512,4096]{1,0:T(8,128)}, u32[]{:S(2)}, u32[]{:S(2)}) %collective-permute-start) | collective-permute-done | bytes 8388640 | tf_op jit(solution)/shard_map/ppermute | solution.py:56
  56.9 11.1 %add.125 = f32[512,4096]{1,0:T(8,128)} add(f32[512,4096]{1,0:T(8,128)} %copy-done.3, f32[512,4096]{1,0:T(8,128)} %collective-permute-done) | non-fusion elementwise | flops 2097152 | bytes 25165824 | tf_op jit(solution)/shard_map/add | solution.py:56
  68.0 0.4 collective-permute-start.1
  68.4 182.4 %collective-permute-done.1 = f32[512,4096]{1,0:T(8,128)} collective-permute-done((f32[512,4096]{1,0:T(8,128)}, f32[512,4096]{1,0:T(8,128)}, u32[]{:S(2)}, u32[]{:S(2)}) %collective-permute-start.1) | collective-permute-done | bytes 8388640 | tf_op jit(solution)/shard_map/ppermute | solution.py:56
  250.8 11.1 %add.126 = f32[512,4096]{1,0:T(8,128)} add(f32[512,4096]{1,0:T(8,128)} %add.125, f32[512,4096]{1,0:T(8,128)} %collective-permute-done.1) | non-fusion elementwise | flops 2097152 | bytes 25165824 | tf_op jit(solution)/shard_map/add | solution.py:56
  261.9 2.3 collective-permute-start.2
  264.4 0.2 convert_reduce_fusion
  264.7 0.1 all_to_all.13
  264.8 16.9 %all_to_all.20 = s32[32,1,2]{2,1,0:T(1,128)S(1)} all-to-all(s32[32,1,2]{2,1,0:T(1,128)S(1)} %bitcast.88), channel_id=1, replica_groups=mesh['seq'=32,'head'=8] {'seq'}, dimensions={0} | all-to-all | bytes 512 | tf_op jit(solution)/shard_map/all_to_all | solution.py:80
  281.8 0.1 copy.116
  281.9 0.1 reshape.298
  282.0 0.1 copy.107
  282.2 64.4 %all-gather.2.cloned.1.call-done = bf16[4096,2,2,128]{3,2,1,0:T(2,128)(2,1)} async-done(((bf16[128,2,2,128]{3,2,1,0:T(2,128)(2,1)}), bf16[4096,2,2,128]{3,2,1,0:T(2,128)(2,1)}) %all-gather.2.cloned.1.call-update) | async-done | bytes 4194320 | tf_op jit(solution)/shard_map/all_gather | solution.py:59
  346.6 7.2 %reshape.289 = bf16[4096,512]{1,0:T(8,128)(2,1)} reshape(bf16[4096,2,2,128]{3,2,1,0:T(2,128)(2,1)} %all-gather.2.cloned.1.call-done) | data formatting | bytes 8388608 | tf_op jit(solution)/shard_map/reshape | solution.py:62
  353.8 91.6 %collective-permute-done.2 = f32[512,4096]{1,0:T(8,128)} collective-permute-done((f32[512,4096]{1,0:T(8,128)}, f32[512,4096]{1,0:T(8,128)}, u32[]{:S(2)}, u32[]{:S(2)}) %collective-permute-start.2) | collective-permute-done | bytes 8388640 | tf_op jit(solution)/shard_map/ppermute | solution.py:56
  445.4 8.1 %multiply_reduce_fusion = (f32[512]{0:T(512)S(1)}, f32[512,4096]{1,0:T(8,128)S(1)}) fusion(f32[512,4096]{1,0:T(8,128)} %add.126, f32[512,4096]{1,0:T(8,128)} %collective-permute-done.2, bf16[4,128,4096]{2,1,0:T(8,128)(2,1)} %param.8), kind=kLoop, calls=%fused_computation.7 | loop fusion | flops 10485248 | bytes 29362176 | tf_op jit(solution)/shard_map/reduce_sum | solution.py:19
  453.6 2.4 fusion.7
  456.0 0.1 reshape.290
  456.1 18.3 %gather_fusion = bf16[64,128,2,2,128]{4,3,2,1,0:T(2,128)(2,1)} fusion(bf16[4,128,2,2,128]{4,3,2,1,0:T(2,128)(2,1)S(1)} %reshape.290, s32[1024]{0:T(1024)S(1)} %pad_clamp_fusion.1), kind=kCustom, calls=%fused_computation | custom fusion | bytes 16777472 | tf_op jit(solution)/shard_map/jit(_take)/gather | solution.py:79
  474.4 7.7 %copy_select_fusion = bf16[32,2,128,2,2,128]{5,2,4,3,1,0:T(8,128)(2,1)} fusion(bf16[32,2,128,2,2,128]{5,4,3,2,1,0:T(2,128)(2,1)} %bitcast.80, pred[32,2]{1,0:T(8,128)(4,1)S(1)} %copy.107), kind=kLoop, calls=%fused_computation.5 | loop fusion | flops 4194304 | bytes 16777280 | tf_op jit(solution)/shard_map/jit(_take)/select_n | solution.py:79
  482.2 10.4 %all-to-all-start.1 = ((bf16[32,2,128,2,2,128]{5,2,4,3,1,0:T(8,128)(2,1)}), bf16[32,2,128,2,2,128]{5,2,4,3,1,0:T(8,128)(2,1)}, u32[]{:S(2)}, u32[]{:S(2)}) async-start(bf16[32,2,128,2,2,128]{5,2,4,3,1,0:T(8,128)(2,1)} %copy_select_fusion), calls=%async_computation.1 | async-start | bytes 16777216 | tf_op jit(solution)/shard_map/all_to_all | solution.py:82
  493.2 0.2 maximum_maximum_fusion
  493.4 179.1 %all-to-all-done.1 = bf16[32,2,128,2,2,128]{5,2,4,3,1,0:T(8,128)(2,1)} async-done(((bf16[32,2,128,2,2,128]{5,2,4,3,1,0:T(8,128)(2,1)}), bf16[32,2,128,2,2,128]{5,2,4,3,1,0:T(8,128)(2,1)}, u32[]{:S(2)}, u32[]{:S(2)}) %all-to-all-start.1) | async-done | bytes 8388640 | tf_op jit(solution)/shard_map/all_to_all | solution.py:82
  672.6 4.3 gather_fusion.1
  676.9 0.1 copy.121
  677.2 3.3 collective-permute-start.3
  680.5 1.6 copy_select_fusion.1
  682.1 5.5 collective-permute-done.3
  687.5 3.1 fusion.56
  690.6 2.0 fusion.16
  692.7 1.0 copy.126
  (47 shorter events, 1.2 us)
Async XLA Ops:
  6.5 32.5 %copy-start = (bf16[2,128,4096]{2,1,0:T(8,128)(2,1)S(1)}, bf16[2,128,4096]{2,1,0:T(8,128)(2,1)}, u32[]{:S(2)}) copy-start(bf16[2,128,4096]{2,1,0:T(8,128)(2,1)} %param.10) | copy-start | bytes 6291460
  6.5 340.0 %all-gather.2.cloned.1.call-start = ((), (), s32[]{:S(2)}) async-start(), calls=%async_computation.2 | async-start | bytes 4325376 | tf_op jit(solution)/shard_map/all_gather | solution.py:59
  6.5 19.6 %copy-start.7 = (f32[4096]{0:T(1024)S(1)}, f32[4096]{0:T(1024)}, u32[]{:S(2)}) copy-start(f32[4096]{0:T(1024)} %param.12) | copy-start | bytes 49156
  22.9 3.4 copy-start.2
  26.4 2.8 copy-start.4
  40.3 3.2 copy-start.3
  43.6 13.3 %collective-permute-start = (f32[512,4096]{1,0:T(8,128)S(1)}, f32[512,4096]{1,0:T(8,128)}, u32[]{:S(2)}, u32[]{:S(2)}) collective-permute-start(f32[512,4096]{1,0:T(8,128)S(1)} %fusion.22), channel_id=1, source_target_pairs={{0,1},{1,0},{2,3},{3,2},{4,5},{5,4},{6,7},{7,6},{8,9},{9,8},{10,11... | collective-permute-start | bytes 25165832 | tf_op jit(solution)/shard_map/ppermute | solution.py:56
  68.0 196.3 %copy-start.8 = (s32[8,2]{0,1:T(2,128)S(1)}, s32[8,2]{0,1:T(2,128)}, u32[]{:S(2)}) copy-start(s32[8,2]{0,1:T(2,128)} %param.15) | copy-start | bytes 196
  68.0 182.8 %collective-permute-start.1 = (f32[512,4096]{1,0:T(8,128)}, f32[512,4096]{1,0:T(8,128)}, u32[]{:S(2)}, u32[]{:S(2)}) collective-permute-start(f32[512,4096]{1,0:T(8,128)} %add.125), channel_id=1, source_target_pairs={{0,2},{1,3},{2,0},{3,1},{4,6},{5,7},{6,4},{7,5},{8,10},{9,11},{10,... | collective-permute-start | bytes 25165832 | tf_op jit(solution)/shard_map/ppermute | solution.py:56
  261.9 183.5 %collective-permute-start.2 = (f32[512,4096]{1,0:T(8,128)}, f32[512,4096]{1,0:T(8,128)}, u32[]{:S(2)}, u32[]{:S(2)}) collective-permute-start(f32[512,4096]{1,0:T(8,128)} %add.126), channel_id=1, source_target_pairs={{0,4},{1,5},{2,6},{3,7},{4,0},{5,1},{6,2},{7,3},{8,12},{9,13},{10,... | collective-permute-start | bytes 25165832 | tf_op jit(solution)/shard_map/ppermute | solution.py:56
  353.8 99.8 %copy-start.5 = (bf16[4096,512]{1,0:T(8,128)(2,1)S(1)}, bf16[4096,512]{1,0:T(8,128)(2,1)}, u32[]{:S(2)}) copy-start(bf16[4096,512]{1,0:T(8,128)(2,1)} %reshape.289) | copy-start | bytes 12582916
  353.8 99.8 %copy-start.9 = (f32[4096]{0:T(1024)S(1)}, f32[4096]{0:T(1024)}, u32[]{:S(2)}) copy-start(f32[4096]{0:T(1024)} %param.13) | copy-start | bytes 49156
  482.2 10.8 %copy-start.6 = (bf16[512,2,128]{2,1,0:T(2,128)(2,1)S(1)}, bf16[512,2,128]{2,1,0:T(2,128)(2,1)}, u32[]{:S(2)}) copy-start(bf16[512,2,128]{2,1,0:T(2,128)(2,1)} %param.14) | copy-start | bytes 786436
  482.2 190.4 %all-to-all-start.1 = ((bf16[32,2,128,2,2,128]{5,2,4,3,1,0:T(8,128)(2,1)}), bf16[32,2,128,2,2,128]{5,2,4,3,1,0:T(8,128)(2,1)}, u32[]{:S(2)}, u32[]{:S(2)}) async-start(bf16[32,2,128,2,2,128]{5,2,4,3,1,0:T(8,128)(2,1)} %copy_select_fusion), calls=%async_computation.1 | async-start | bytes 16777216 | tf_op jit(solution)/shard_map/all_to_all | solution.py:82
  677.2 10.4 %collective-permute-start.3 = (bf16[1,256,2,2,128]{4,1,2,0,3:T(8,128)(2,1)S(1)}, bf16[1,256,2,2,128]{4,1,2,0,3:T(8,128)(2,1)S(1)}, u32[]{:S(2)}, u32[]{:S(2)}) collective-permute-start(bf16[1,256,2,2,128]{4,1,2,0,3:T(8,128)(2,1)S(1)} %bitcast.87), channel_id=1, source_target_pairs={{0,8},{8,16},{16,24},{24,32},{32,40},{40,48},{48,56},{56,64},{64,7... | collective-permute-start | bytes 786440 | tf_op jit(solution)/shard_map/ppermute | solution.py:15
  687.5 6.1 copy-start.1
Sparse Core Ops, SparseCore 0:
  264.4 82.1 all-gather.1
